TPU v7x, 32 devices: a whole 2x2x4 slice. The times are simulated.
32 devices in a mesh: dp: 4 (over y, x), expert: 8 (over z, core).
Axes of the slice: x: 2, y: 2, z: 4, core: 2. Of those that a mesh axis runs over, the one named last changes fastest.
Arguments:
- features: float32 [32768, 256], P(('dp', 'expert')), may hold values from -6 to 6
- cotangent: float32 [32768, 512], P(('dp', 'expert')), may hold values from -6 to 6
- routes: int32 [32768, 8], P(('dp', 'expert')), may hold values from 0 to 15, all different within a row; in each aligned block of 256 rows (0 to 255, 256 to 511, ...) at most 192 rows name the same one
- lengths: int32 [32, 16], P(('dp', 'expert')), may hold values from 1 to 200, 1024 in all within a row
- gate_weight: float32 [256, 40], replicated, may hold values from -0.1875 to 0.1875
- first_weight: float32 [16, 256, 256], P('expert', 'dp'), may hold values from -0.375 to 0.375
- second_weight: float32 [16, 256, 256], P('expert', 'dp'), may hold values from -0.75 to 0.75
- expert_bias: float32 [16, 512], P('expert', 'dp'), may hold values from -0.625 to 0.625
- gate_momentum: float32 [256, 40], replicated, may hold values from -12 to 12
- gate_average: float32 [256, 40], replicated, may hold values from -0.1875 to 0.1875
- first_momentum: float32 [16, 256, 256], P('expert', 'dp'), may hold values from -1.25 to 1.25
- first_average: float32 [16, 256, 256], P('expert', 'dp'), may hold values from -0.375 to 0.375
- second_momentum: float32 [16, 256, 256], P('expert', 'dp'), may hold values from -0.625 to 0.625
- second_average: float32 [16, 256, 256], P('expert', 'dp'), may hold values from -0.75 to 0.75
- bias_momentum: float32 [16, 512], P('expert', 'dp'), may hold values from -1.25 to 1.25
- bias_average: float32 [16, 512], P('expert', 'dp'), may hold values from -0.625 to 0.625
Outputs:
- task_outputs: float32 [32768, 512], P(('dp', 'expert'))
- input_grad: float32 [32768, 256], P(('dp', 'expert'))
- gate_momentum_new: float32 [256, 40], replicated
- gate_weight_new: float32 [256, 40], replicated
- gate_average_new: float32 [256, 40], replicated
- first_momentum_new: float32 [16, 256, 256], P('expert', 'dp')
- first_weight_new: float32 [16, 256, 256], P('expert', 'dp')
- first_average_new: float32 [16, 256, 256], P('expert', 'dp')
- second_momentum_new: float32 [16, 256, 256], P('expert', 'dp')
- second_weight_new: float32 [16, 256, 256], P('expert', 'dp')
- second_average_new: float32 [16, 256, 256], P('expert', 'dp')
- bias_momentum_new: float32 [16, 512], P('expert', 'dp')
- bias_new: float32 [16, 512], P('expert', 'dp')
- bias_average_new: float32 [16, 512], P('expert', 'dp')
Inputs may be any that keep to these rules, and one draw needn't show every extreme that they name: `routes`: each row names 8 different experts: the first 4 are task 0's selectors, the next 4 task 1's. In each aligned block of 256 rows (one micro-batch of one device) no expert is named by more than 192 rows, and in some block one expert is named by exactly 192 rows. `lengths`: the sessions of one device cover its 1024 rows in order and never cross devices; the longest has the maximum length.
All inputs are finite; a program needn't handle non-finite values.
Results may differ from a plain program's by a relative error of at most 0.002.
Values sent between devices are 32-bit elements; how exact they have to be, the bound alone decides.
A program may use at most 192 MiB of HBM per device.

v0:
```python
import math
import jax
import jax.numpy as jnp
from jax import lax
from jax.sharding import PartitionSpec as P

D = 256
HID = 256
DOUT = 256
EXPERTS = 16
BITS = 4
TASKS = 2
SELECT = 4
MICRO = 4
CAP = 192
HIGHEST = lax.Precision.HIGHEST
OFFSET = 3.5
SHARPNESS = 10.0
MOMENTUM = 0.5
AVERAGE_DECAY = 0.5
EXPERT_RATE = 0.4
GATE_RATE = 0.01


def smooth_step(argument):
    clipped = jnp.clip(argument, -0.5 * SHARPNESS, 0.5 * SHARPNESS)
    return -2.0 / SHARPNESS**3 * clipped**3 + 1.5 / SHARPNESS * clipped + 0.5


def gate_strengths(features, gate_weight, lengths_row, chosen):
    row_count = features.shape[0]
    session_ends = jnp.cumsum(lengths_row, dtype=jnp.int32)
    starts = session_ends - lengths_row
    places = jnp.arange(row_count, dtype=jnp.int32)[:, None]
    member = ((places >= starts[None, :]) & (places < session_ends[None, :])).astype(jnp.float32)
    session_sums = jnp.dot(member.T, features, precision=HIGHEST)
    session_means = session_sums / lengths_row.astype(jnp.float32)[:, None]
    context = features + jnp.dot(member, session_means, precision=HIGHEST)
    logits = jnp.dot(context, gate_weight, precision=HIGHEST).reshape(
        row_count, TASKS, SELECT, BITS + 1
    )
    weights = jax.nn.softmax(logits[..., 0], axis=-1)
    powers = 2 ** jnp.arange(BITS, dtype=jnp.int32)
    code_bits = chosen.reshape(row_count, TASKS, SELECT)[..., None] // powers % 2
    code_signs = 2.0 * code_bits.astype(jnp.float32) - 1.0
    strength = jnp.prod(smooth_step(code_signs * logits[..., 1:] + OFFSET), axis=-1)
    return (weights * strength).reshape(row_count, TASKS * SELECT)


def slot_index(chosen):
    destination = chosen.reshape(-1)
    matches = (destination[:, None] == jnp.arange(EXPERTS, dtype=jnp.int32)[None, :]).astype(
        jnp.int32
    )
    before = jnp.cumsum(matches, axis=0, dtype=jnp.int32) - matches
    position = jnp.sum(before * matches, axis=1, dtype=jnp.int32)
    return destination * CAP + position


def expert_forward(slot_rows, first_full, second_full, bias_full):
    pre_act = (
        jnp.einsum("sjcd,jdh->sjch", slot_rows, first_full, precision=HIGHEST)
        + bias_full[None, :, None, :HID]
    )
    hidden = jax.nn.relu(pre_act)
    slot_out = (
        jnp.einsum("sjch,jho->sjco", hidden, second_full, precision=HIGHEST)
        + bias_full[None, :, None, HID:]
    )
    return (pre_act, hidden, slot_out)


def expert_backward(slot_rows, pre_act, hidden, slot_cot, first_full, second_full):
    second_delta = jnp.einsum("sjch,sjco->jho", hidden, slot_cot, precision=HIGHEST)
    hidden_cot = jnp.einsum("sjco,jho->sjch", slot_cot, second_full, precision=HIGHEST) * (
        pre_act > 0.0
    ).astype(jnp.float32)
    first_delta = jnp.einsum("sjcd,sjch->jdh", slot_rows, hidden_cot, precision=HIGHEST)
    bias_delta = jnp.concatenate(
        [jnp.sum(hidden_cot, axis=(0, 2)), jnp.sum(slot_cot, axis=(0, 2))], axis=-1
    )
    slot_back = jnp.einsum("sjch,jdh->sjcd", hidden_cot, first_full, precision=HIGHEST)
    return (slot_back, (first_delta, second_delta, bias_delta))


def apply_update(weight, gradient, momentum, average, step_rate):
    momentum_new = MOMENTUM * momentum + gradient
    weight_new = weight - step_rate * (gradient + MOMENTUM * momentum_new)
    average_new = AVERAGE_DECAY * average + (1.0 - AVERAGE_DECAY) * weight_new
    return (momentum_new, weight_new, average_new)


def local(
    features,
    cotangent,
    routes,
    lengths,
    gate_weight,
    first_weight,
    second_weight,
    expert_bias,
    gate_momentum,
    gate_average,
    first_momentum,
    first_average,
    second_momentum,
    second_average,
    bias_momentum,
    bias_average,
):
    row_count = features.shape[0]
    pair_count = TASKS * SELECT
    micro_rows = row_count // MICRO

    def gate_part(rows_in, weight_in):
        return gate_strengths(rows_in, weight_in, lengths[0], routes)

    gate_terms, gate_pull = jax.vjp(gate_part, features, gate_weight)
    pair_cot = jnp.broadcast_to(
        cotangent.reshape(row_count, TASKS, 1, DOUT), (row_count, TASKS, SELECT, DOUT)
    ).reshape(row_count, pair_count, DOUT)
    pair_grads = gate_terms[:, :, None] * pair_cot
    local_count = first_weight.shape[0]
    first_sum = jnp.zeros((local_count, D, HID), jnp.float32)
    second_sum = jnp.zeros((local_count, HID, DOUT), jnp.float32)
    bias_sum = jnp.zeros((local_count, HID + DOUT), jnp.float32)
    output_parts = []
    input_parts = []
    cot_parts = []
    for micro_index in range(MICRO):
        begin = micro_index * micro_rows
        first_full = lax.all_gather(first_weight, "dp", axis=1, tiled=True)
        second_full = lax.all_gather(second_weight, "dp", axis=1, tiled=True)
        bias_full = lax.all_gather(expert_bias, "dp", axis=1, tiled=True)
        rows_now = features[begin : begin + micro_rows]
        slot_place = slot_index(routes[begin : begin + micro_rows])
        send_rows = (
            jnp.zeros((EXPERTS * CAP, D), jnp.float32)
            .at[slot_place]
            .set(jnp.repeat(rows_now, pair_count, axis=0))
            .reshape(EXPERTS, CAP, D)
        )
        send_grads = (
            jnp.zeros((EXPERTS * CAP, DOUT), jnp.float32)
            .at[slot_place]
            .set(pair_grads[begin : begin + micro_rows].reshape(-1, DOUT))
            .reshape(EXPERTS, CAP, DOUT)
        )
        got_rows = lax.all_to_all(send_rows, "expert", split_axis=0, concat_axis=0, tiled=True)
        slot_rows = got_rows.reshape(-1, local_count, CAP, D)
        pre_act, hidden, slot_out = expert_forward(slot_rows, first_full, second_full, bias_full)
        returned_out = lax.all_to_all(
            slot_out.reshape(EXPERTS, CAP, DOUT), "expert", split_axis=0, concat_axis=0, tiled=True
        )
        got_grads = lax.all_to_all(send_grads, "expert", split_axis=0, concat_axis=0, tiled=True)
        slot_back, deltas = expert_backward(
            slot_rows,
            pre_act,
            hidden,
            got_grads.reshape(-1, local_count, CAP, DOUT),
            first_full,
            second_full,
        )
        returned_back = lax.all_to_all(
            slot_back.reshape(EXPERTS, CAP, D), "expert", split_axis=0, concat_axis=0, tiled=True
        )
        first_sum = first_sum + deltas[0]
        second_sum = second_sum + deltas[1]
        bias_sum = bias_sum + deltas[2]
        picked = returned_out.reshape(EXPERTS * CAP, DOUT)[slot_place].reshape(
            micro_rows, TASKS, SELECT, DOUT
        )
        combined = jnp.sum(
            gate_terms[begin : begin + micro_rows].reshape(micro_rows, TASKS, SELECT, 1) * picked,
            axis=2,
        )
        output_parts.append(combined.reshape(micro_rows, TASKS * DOUT))
        cot_parts.append(
            jnp.sum(
                pair_cot[begin : begin + micro_rows] * picked.reshape(micro_rows, pair_count, DOUT),
                axis=-1,
            )
        )
        input_parts.append(
            jnp.sum(
                returned_back.reshape(EXPERTS * CAP, D)[slot_place].reshape(
                    micro_rows, pair_count, D
                ),
                axis=1,
            )
        )
    task_outputs = jnp.concatenate(output_parts, axis=0)
    rows_from_gate, gate_local = gate_pull(jnp.concatenate(cot_parts, axis=0))
    input_grad = rows_from_gate + jnp.concatenate(input_parts, axis=0)
    gate_grad = lax.psum(gate_local, ("dp", "expert"))
    first_grad, second_grad, bias_grad = (
        lax.psum_scatter(first_sum, "dp", scatter_dimension=1, tiled=True),
        lax.psum_scatter(second_sum, "dp", scatter_dimension=1, tiled=True),
        lax.psum_scatter(bias_sum, "dp", scatter_dimension=1, tiled=True),
    )
    grad_scale = 1.0 / math.sqrt(row_count * lax.axis_size("dp") * lax.axis_size("expert"))
    gate_new = apply_update(
        gate_weight, gate_grad * grad_scale, gate_momentum, gate_average, GATE_RATE
    )
    first_new = apply_update(
        first_weight, first_grad * grad_scale, first_momentum, first_average, EXPERT_RATE
    )
    second_new = apply_update(
        second_weight, second_grad * grad_scale, second_momentum, second_average, EXPERT_RATE
    )
    bias_new = apply_update(
        expert_bias, bias_grad * grad_scale, bias_momentum, bias_average, EXPERT_RATE
    )
    return (
        task_outputs,
        input_grad,
        gate_new[0],
        gate_new[1],
        gate_new[2],
        first_new[0],
        first_new[1],
        first_new[2],
        second_new[0],
        second_new[1],
        second_new[2],
        bias_new[0],
        bias_new[1],
        bias_new[2],
    )


def solution(mesh):
    placed = (
        P(("dp", "expert"), None),
        P(("dp", "expert"), None),
        P(("dp", "expert"), None),
        P(("dp", "expert"), None),
        P(),
        P("expert", "dp", None),
        P("expert", "dp", None),
        P("expert", "dp"),
        P(),
        P(),
        P("expert", "dp", None),
        P("expert", "dp", None),
        P("expert", "dp", None),
        P("expert", "dp", None),
        P("expert", "dp"),
        P("expert", "dp"),
    )
    return jax.shard_map(
        local,
        mesh=mesh,
        in_specs=placed,
        out_specs=(
            P(("dp", "expert"), None),
            P(("dp", "expert"), None),
            P(),
            P(),
            P(),
            P("expert", "dp", None),
            P("expert", "dp", None),
            P("expert", "dp", None),
            P("expert", "dp", None),
            P("expert", "dp", None),
            P("expert", "dp", None),
            P("expert", "dp"),
            P("expert", "dp"),
            P("expert", "dp"),
        ),
        check_vma=False,
    )
```

profile of v0, /device:TPU:0, one launch (start us, length us, event | category | flops | bytes accessed | tf_op | source)
XLA Modules:
  0.0 1447.1 jit_solution(313344892652982760)
XLA Ops:
  16.6 10.9 scatter_custom_fusion
  53.4 11.3 scatter_custom_fusion.3
  64.7 40.7 %all-to-all-done = f32[16,192,256]{2,1,0:T(8,128)S(1)} async-done(((f32[16,192,256]{2,1,0:T(8,128)}), f32[16,192,256]{2,1,0:T(8,128)S(1)}, u32[]{:S(2)}, u32[]{:S(2)}) %all-to-all-start) | async-done | bytes 3145760 | tf_op jit(solution)/shard_map/all_to_all | solution.py:149
  130.3 11.2 scatter_custom_fusion.2
  141.6 40.6 %all-to-all-done.6 = f32[16,192,256]{2,1,0:T(8,128)S(1)} async-done(((f32[16,192,256]{2,1,0:T(8,128)}), f32[16,192,256]{2,1,0:T(8,128)S(1)}, u32[]{:S(2)}, u32[]{:S(2)}) %all-to-all-start.6) | async-done | bytes 3145760 | tf_op jit(solution)/shard_map/all_to_all | solution.py:149
  194.5 10.9 scatter_custom_fusion.1
  205.4 54.6 %all-to-all-done.4 = f32[16,192,256]{2,1,0:T(8,128)} async-done(((f32[16,192,256]{2,1,0:T(8,128)}), f32[16,192,256]{2,1,0:T(8,128)}, u32[]{:S(2)}, u32[]{:S(2)}) %all-to-all-start.4) | async-done | bytes 3145760 | tf_op jit(solution)/shard_map/all_to_all | solution.py:149
  272.0 10.7 all_gather.6
  302.2 33.1 %all-to-all-done.2 = f32[16,192,256]{2,1,0:T(8,128)S(1)} async-done(((f32[16,192,256]{2,1,0:T(8,128)}), f32[16,192,256]{2,1,0:T(8,128)S(1)}, u32[]{:S(2)}, u32[]{:S(2)}) %all-to-all-start.2) | async-done | bytes 3145760 | tf_op jit(solution)/shard_map/all_to_all | solution.py:149
  351.1 61.2 %all-to-all-done.1 = f32[16,192,256]{2,1,0:T(8,128)S(1)} async-done(((f32[16,192,256]{2,1,0:T(8,128)}), f32[16,192,256]{2,1,0:T(8,128)S(1)}, u32[]{:S(2)}, u32[]{:S(2)}) %all-to-all-start.1) | async-done | bytes 3145760 | tf_op jit(solution)/shard_map/all_to_all | solution.py:152
  427.6 61.2 %all-to-all-done.7 = f32[16,192,256]{2,1,0:T(8,128)} async-done(((f32[16,192,256]{2,1,0:T(8,128)}), f32[16,192,256]{2,1,0:T(8,128)}, u32[]{:S(2)}, u32[]{:S(2)}) %all-to-all-start.7) | async-done | bytes 3145760 | tf_op jit(solution)/shard_map/all_to_all | solution.py:152
  503.7 61.3 %all-to-all-done.5 = f32[16,192,256]{2,1,0:T(8,128)} async-done(((f32[16,192,256]{2,1,0:T(8,128)}), f32[16,192,256]{2,1,0:T(8,128)}, u32[]{:S(2)}, u32[]{:S(2)}) %all-to-all-start.5) | async-done | bytes 3145760 | tf_op jit(solution)/shard_map/all_to_all | solution.py:152
  698.7 11.5 scatter_custom_fusion.7
  715.7 11.5 scatter_custom_fusion.6
  727.2 60.0 %all-to-all-done.14 = f32[16,192,256]{2,1,0:T(8,128)S(1)} async-done(((f32[16,192,256]{2,1,0:T(8,128)}), f32[16,192,256]{2,1,0:T(8,128)S(1)}, u32[]{:S(2)}, u32[]{:S(2)}) %all-to-all-start.14) | async-done | bytes 3145760 | tf_op jit(solution)/shard_map/all_to_all | solution.py:155
  793.5 11.4 scatter_custom_fusion.5
  804.9 60.1 %all-to-all-done.12 = f32[16,192,256]{2,1,0:T(8,128)} async-done(((f32[16,192,256]{2,1,0:T(8,128)}), f32[16,192,256]{2,1,0:T(8,128)}, u32[]{:S(2)}, u32[]{:S(2)}) %all-to-all-start.12) | async-done | bytes 3145760 | tf_op jit(solution)/shard_map/all_to_all | solution.py:155
  868.7 11.5 scatter_custom_fusion.4
  880.2 60.0 %all-to-all-done.10 = f32[16,192,256]{2,1,0:T(8,128)S(1)} async-done(((f32[16,192,256]{2,1,0:T(8,128)}), f32[16,192,256]{2,1,0:T(8,128)S(1)}, u32[]{:S(2)}, u32[]{:S(2)}) %all-to-all-start.10) | async-done | bytes 3145760 | tf_op jit(solution)/shard_map/all_to_all | solution.py:155
  957.4 60.8 %all-to-all-done.8 = f32[16,192,256]{2,1,0:T(8,128)} async-done(((f32[16,192,256]{2,1,0:T(8,128)}), f32[16,192,256]{2,1,0:T(8,128)}, u32[]{:S(2)}, u32[]{:S(2)}) %all-to-all-start.8) | async-done | bytes 3145760 | tf_op jit(solution)/shard_map/all_to_all | solution.py:155
  1033.9 59.7 %all-to-all-done.15 = f32[16,192,256]{2,1,0:T(8,128)S(1)} async-done(((f32[16,192,256]{2,1,0:T(8,128)}), f32[16,192,256]{2,1,0:T(8,128)S(1)}, u32[]{:S(2)}, u32[]{:S(2)}) %all-to-all-start.15) | async-done | bytes 3145760 | tf_op jit(solution)/shard_map/all_to_all | solution.py:164
  1110.0 59.8 %all-to-all-done.13 = f32[16,192,256]{2,1,0:T(8,128)} async-done(((f32[16,192,256]{2,1,0:T(8,128)}), f32[16,192,256]{2,1,0:T(8,128)}, u32[]{:S(2)}, u32[]{:S(2)}) %all-to-all-start.13) | async-done | bytes 3145760 | tf_op jit(solution)/shard_map/all_to_all | solution.py:164
  1243.9 41.1 %psum.7 = f32[256,40]{0,1:T(8,128)S(1)} all-reduce(f32[256,40]{0,1:T(8,128)S(1)} %fusion.258), channel_id=1, replica_groups=mesh['dp'=4,'expert'=8] {'dp','expert'}, use_global_device_ids=true, to_apply=%region_36.37 | all-reduce | flops 10240 | bytes 81920 | tf_op jit(solution)/shard_map/psum | solution.py:195
  1374.8 17.6 %reduce-scatter.6.cloned.1.call-done = f32[2,64,256]{2,1,0:T(8,128)} async-done(((f32[2,256,256]{2,1,0:T(8,128)}), f32[2,64,256]{2,1,0:T(8,128)}) %reduce-scatter.6.cloned.1.call-update) | async-done | bytes 131088 | tf_op jit(solution)/shard_map/reduce_scatter | solution.py:197
  (429 shorter events, 558.6 us)
Async XLA Ops:
  27.5 77.9 %all-to-all-start = ((f32[16,192,256]{2,1,0:T(8,128)}), f32[16,192,256]{2,1,0:T(8,128)S(1)}, u32[]{:S(2)}, u32[]{:S(2)}) async-start(f32[16,192,256]{2,1,0:T(8,128)} %bitcast.394), calls=%async_computation | async-start | bytes 6291456 | tf_op jit(solution)/shard_map/all_to_all | solution.py:149
  53.4 53.7 %copy-start.71 = (s32[2048,1]{0,1:T(1,128)}, s32[2048,1]{0,1:T(1,128)S(1)}, u32[]{:S(2)}) copy-start(s32[2048,1]{0,1:T(1,128)S(1)} %compare_select_fusion) | copy-start | bytes 24580
  107.1 75.1 %all-to-all-start.6 = ((f32[16,192,256]{2,1,0:T(8,128)}), f32[16,192,256]{2,1,0:T(8,128)S(1)}, u32[]{:S(2)}, u32[]{:S(2)}) async-start(f32[16,192,256]{2,1,0:T(8,128)} %bitcast.393), calls=%async_computation.6 | async-start | bytes 6291456 | tf_op jit(solution)/shard_map/all_to_all | solution.py:149
  130.3 51.9 %copy-start.73 = (s32[2048,1]{0,1:T(1,128)}, s32[2048,1]{0,1:T(1,128)S(1)}, u32[]{:S(2)}) copy-start(s32[2048,1]{0,1:T(1,128)S(1)} %compare_select_fusion.1) | copy-start | bytes 24580
  183.9 76.2 %all-to-all-start.4 = ((f32[16,192,256]{2,1,0:T(8,128)}), f32[16,192,256]{2,1,0:T(8,128)}, u32[]{:S(2)}, u32[]{:S(2)}) async-start(f32[16,192,256]{2,1,0:T(8,128)} %bitcast.392), calls=%async_computation.4 | async-start | bytes 6291456 | tf_op jit(solution)/shard_map/all_to_all | solution.py:149
  194.5 65.6 %copy-start.75 = (s32[2048,1]{0,1:T(1,128)}, s32[2048,1]{0,1:T(1,128)S(1)}, u32[]{:S(2)}) copy-start(s32[2048,1]{0,1:T(1,128)S(1)} %compare_select_fusion.2) | copy-start | bytes 24580
  260.1 22.6 %copy-start.43 = (f32[2,64,256]{2,1,0:T(8,128)S(1)}, f32[2,64,256]{2,1,0:T(8,128)}, u32[]{:S(2)}) copy-start(f32[2,64,256]{2,1,0:T(8,128)} %param.22) | copy-start | bytes 393220
  260.1 75.3 %all-to-all-start.2 = ((f32[16,192,256]{2,1,0:T(8,128)}), f32[16,192,256]{2,1,0:T(8,128)S(1)}, u32[]{:S(2)}, u32[]{:S(2)}) async-start(f32[16,192,256]{2,1,0:T(8,128)} %bitcast.395), calls=%async_computation.2 | async-start | bytes 6291456 | tf_op jit(solution)/shard_map/all_to_all | solution.py:149
  337.0 75.4 %all-to-all-start.1 = ((f32[16,192,256]{2,1,0:T(8,128)}), f32[16,192,256]{2,1,0:T(8,128)S(1)}, u32[]{:S(2)}, u32[]{:S(2)}) async-start(f32[16,192,256]{2,1,0:T(8,128)} %bitcast.399), calls=%async_computation.1 | async-start | bytes 6291456 | tf_op jit(solution)/shard_map/all_to_all | solution.py:152
  412.3 76.5 %all-to-all-start.7 = ((f32[16,192,256]{2,1,0:T(8,128)}), f32[16,192,256]{2,1,0:T(8,128)}, u32[]{:S(2)}, u32[]{:S(2)}) async-start(f32[16,192,256]{2,1,0:T(8,128)} %bitcast.400), calls=%async_computation.7 | async-start | bytes 6291456 | tf_op jit(solution)/shard_map/all_to_all | solution.py:152
  488.8 76.2 %all-to-all-start.5 = ((f32[16,192,256]{2,1,0:T(8,128)}), f32[16,192,256]{2,1,0:T(8,128)}, u32[]{:S(2)}, u32[]{:S(2)}) async-start(f32[16,192,256]{2,1,0:T(8,128)} %bitcast.398), calls=%async_computation.5 | async-start | bytes 6291456 | tf_op jit(solution)/shard_map/all_to_all | solution.py:152
  565.0 114.0 %all-to-all-start.3 = ((f32[16,192,256]{2,1,0:T(8,128)}), f32[16,192,256]{2,1,0:T(8,128)}, u32[]{:S(2)}, u32[]{:S(2)}) async-start(f32[16,192,256]{2,1,0:T(8,128)} %bitcast.391), calls=%async_computation.3 | async-start | bytes 6291456 | tf_op jit(solution)/shard_map/all_to_all | solution.py:152
  710.2 77.1 %all-to-all-start.14 = ((f32[16,192,256]{2,1,0:T(8,128)}), f32[16,192,256]{2,1,0:T(8,128)S(1)}, u32[]{:S(2)}, u32[]{:S(2)}) async-start(f32[16,192,256]{2,1,0:T(8,128)} %bitcast.404), calls=%async_computation.14 | async-start | bytes 6291456 | tf_op jit(solution)/shard_map/all_to_all | solution.py:155
  789.0 76.0 %all-to-all-start.12 = ((f32[16,192,256]{2,1,0:T(8,128)}), f32[16,192,256]{2,1,0:T(8,128)}, u32[]{:S(2)}, u32[]{:S(2)}) async-start(f32[16,192,256]{2,1,0:T(8,128)} %bitcast.403), calls=%async_computation.12 | async-start | bytes 6291456 | tf_op jit(solution)/shard_map/all_to_all | solution.py:155
  865.0 75.1 %all-to-all-start.10 = ((f32[16,192,256]{2,1,0:T(8,128)}), f32[16,192,256]{2,1,0:T(8,128)S(1)}, u32[]{:S(2)}, u32[]{:S(2)}) async-start(f32[16,192,256]{2,1,0:T(8,128)} %bitcast.402), calls=%async_computation.10 | async-start | bytes 6291456 | tf_op jit(solution)/shard_map/all_to_all | solution.py:155
  941.8 76.4 %all-to-all-start.8 = ((f32[16,192,256]{2,1,0:T(8,128)}), f32[16,192,256]{2,1,0:T(8,128)}, u32[]{:S(2)}, u32[]{:S(2)}) async-start(f32[16,192,256]{2,1,0:T(8,128)} %bitcast.401), calls=%async_computation.8 | async-start | bytes 6291456 | tf_op jit(solution)/shard_map/all_to_all | solution.py:155
  1018.2 75.3 %all-to-all-start.15 = ((f32[16,192,256]{2,1,0:T(8,128)}), f32[16,192,256]{2,1,0:T(8,128)S(1)}, u32[]{:S(2)}, u32[]{:S(2)}) async-start(f32[16,192,256]{2,1,0:T(8,128)} %bitcast.396), calls=%async_computation.15 | async-start | bytes 6291456 | tf_op jit(solution)/shard_map/all_to_all | solution.py:164
  1093.5 76.2 %all-to-all-start.13 = ((f32[16,192,256]{2,1,0:T(8,128)}), f32[16,192,256]{2,1,0:T(8,128)}, u32[]{:S(2)}, u32[]{:S(2)}) async-start(f32[16,192,256]{2,1,0:T(8,128)} %bitcast.397), calls=%async_computation.13 | async-start | bytes 6291456 | tf_op jit(solution)/shard_map/all_to_all | solution.py:164
  1169.7 126.5 %all-to-all-start.11 = ((f32[16,192,256]{2,1,0:T(8,128)}), f32[16,192,256]{2,1,0:T(8,128)}, u32[]{:S(2)}, u32[]{:S(2)}) async-start(f32[16,192,256]{2,1,0:T(8,128)} %bitcast.390), calls=%async_computation.11 | async-start | bytes 6291456 | tf_op jit(solution)/shard_map/all_to_all | solution.py:164
  1296.3 132.1 %all-to-all-start.9 = ((f32[16,192,256]{2,1,0:T(8,128)}), f32[16,192,256]{2,1,0:T(8,128)}, u32[]{:S(2)}, u32[]{:S(2)}) async-start(f32[16,192,256]{2,1,0:T(8,128)} %bitcast.389), calls=%async_computation.9 | async-start | bytes 6291456 | tf_op jit(solution)/shard_map/all_to_all | solution.py:164
  1300.9 70.6 %reduce-scatter.10.cloned.1.call-start = ((), (), s32[]{:S(2)}) async-start(), calls=%async_computation.21 | async-start | bytes 327680
  1311.2 61.8 %reduce-scatter.8.cloned.1.call-start = ((), (), s32[]{:S(2)}) async-start(), calls=%async_computation.20 | async-start | bytes 655360 | tf_op jit(solution)/shard_map/reduce_scatter | solution.py:198
  1338.7 53.7 %reduce-scatter.6.cloned.1.call-start = ((), (), s32[]{:S(2)}) async-start(), calls=%async_computation.19 | async-start | bytes 655360 | tf_op jit(solution)/shard_map/reduce_scatter | solution.py:197
  1368.9 25.4 %copy-start.66 = (s32[2048]{0:T(1024)S(1)}, s32[2048]{0:T(1024)}, u32[]{:S(2)}) copy-start(s32[2048]{0:T(1024)} %broadcast_clamp_fusion) | copy-start | bytes 24580
  (86 other events, 501.4 us)
Sparse Core Ops, SparseCore 0:
  1311.3 25.2 reduce-scatter.9
  1339.7 25.0 reduce-scatter.7
  1367.6 24.7 reduce-scatter.5
where the time goes:
time: 1460 us; the launch traced here: 1450 us
  waiting for transfers between devices  731 us (50%)
  local copies, waits for them, and re-layouts  319 us (22%)
  matrix products  135 us (9%)
  other arithmetic  104 us (7%)
  starting transfers between devices  73.8 us (5%)
  blocking collectives  69.1 us (5%)
  between operations  15.8 us (1%)
    all_to_all x4, waiting for transfers between devices, local(): lax.all_to_all(send_grads, 'expert', split_axis=0, concat_axis=0, tiled=T...  241 us
    all_to_all x4, waiting for transfers between devices, local(): lax.all_to_all(slot_out.reshape(EXPERTS, CAP, DOUT), 'expert', split_axis...  184 us
    all_to_all x4, waiting for transfers between devices, local(): lax.all_to_all(send_rows, 'expert', split_axis=0, concat_axis=0, tiled=True)  169 us
    all_to_all x4, waiting for transfers between devices, local(): lax.all_to_all(slot_back.reshape(EXPERTS, CAP, D), 'expert', split_axis=0...  119 us
    scatter x4, local copies, waits for them, and re-layouts, local(): send_grads = jnp.zeros((EXPERTS * CAP, DOUT), jnp.float32).at[slot_place]...  45.9 us
    scatter x4, local copies, waits for them, and re-layouts, local(): send_rows = jnp.zeros((EXPERTS * CAP, D), jnp.float32).at[slot_place].set...  44.3 us
    psum x1, blocking collectives, local(): gate_grad = lax.psum(gate_local, ('dp', 'expert'))  41.1 us
    gather x4, local copies, waits for them, and re-layouts, local(): returned_back.reshape(EXPERTS * CAP, D)[slot_place]  38.5 us
  transfers between devices with their start and end apart: 19, of which 14 were waited for; matrix products, arithmetic and copies ran while one was open for 33% of the time, Pallas kernels for 0%

commit v1 on v0

--- a/solution.py
+++ b/solution.py
@@ -20,6 +20,22 @@
 AVERAGE_DECAY = 0.5
 EXPERT_RATE = 0.4
 GATE_RATE = 0.01
+
+
+def pairwise_exchange(shard, axis, split, join):
+    ways, here = (lax.axis_size(axis), lax.axis_index(axis))
+    width = shard.shape[split] // ways
+    dims = list(shard.shape)
+    dims[split] = width
+    height = dims[join]
+    dims[join] = height * ways
+    full = jnp.zeros(dims, shard.dtype)
+    for mask in range(ways):
+        part = lax.dynamic_slice_in_dim(shard, (here ^ mask) * width, width, axis=split)
+        if mask:
+            part = lax.ppermute(part, axis, [(d, d ^ mask) for d in range(ways)])
+        full = lax.dynamic_update_slice_in_dim(full, part, (here ^ mask) * height, axis=join)
+    return full
 
 
 def smooth_step(argument):
@@ -146,7 +162,7 @@
             .set(pair_grads[begin : begin + micro_rows].reshape(-1, DOUT))
             .reshape(EXPERTS, CAP, DOUT)
         )
-        got_rows = lax.all_to_all(send_rows, "expert", split_axis=0, concat_axis=0, tiled=True)
+        got_rows = pairwise_exchange(send_rows, "expert", 0, 0)
         slot_rows = got_rows.reshape(-1, local_count, CAP, D)
         pre_act, hidden, slot_out = expert_forward(slot_rows, first_full, second_full, bias_full)
         returned_out = lax.all_to_all(

time: 1460 us -> 1450 us (level)
  starting transfers between devices: 73.8 us -> 128 us
  waiting for transfers between devices: 731 us -> 697 us
    ppermute x0 -> x28, waiting for transfers between devices: none -> 317 us  [pairwise_exchange(): part = lax.ppermute(part, axis, [(d, d ^ mask) for d in range(ways)])]
    all_to_all x4, waiting for transfers between devices: 184 us -> 0.01 us  [local(): lax.all_to_all(slot_out.reshape(EXPERTS, CAP, DOUT), 'expert', split_axis...]
    all_to_all x4 -> x0, waiting for transfers between devices: 169 us -> none  [local(): lax.all_to_all(send_rows, 'expert', split_axis=0, concat_axis=0, tiled=True)]
    ppermute x0 -> x28, starting transfers between devices: none -> 46.5 us  [pairwise_exchange(): part = lax.ppermute(part, axis, [(d, d ^ mask) for d in range(ways)])]
    all_to_all x4, starting transfers between devices: 18.3 us -> 44.2 us  [local(): lax.all_to_all(slot_out.reshape(EXPERTS, CAP, DOUT), 'expert', split_axis...]
    all_to_all x4 -> x0, starting transfers between devices: 18.4 us -> none  [local(): lax.all_to_all(send_rows, 'expert', split_axis=0, concat_axis=0, tiled=True)]
  transfers between devices with their start and end apart: 19 -> 43, of which waited for: 14 -> 21; matrix products, arithmetic and copies ran while one was open for 33% -> 31% of each run, Pallas kernels for 0% -> 0%
where the time goes in v1:
time: 1450 us; the launch traced here: 1440 us
  waiting for transfers between devices  697 us (48%)
  local copies, waits for them, and re-layouts  312 us (22%)
  starting transfers between devices  128 us (9%)
  matrix products  127 us (9%)
  other arithmetic  94.3 us (7%)
  blocking collectives  69.5 us (5%)
  between operations  16.1 us (1%)
    ppermute x28, waiting for transfers between devices, pairwise_exchange(): part = lax.ppermute(part, axis, [(d, d ^ mask) for d in range(ways)])  317 us
    all_to_all x4, waiting for transfers between devices, local(): lax.all_to_all(send_grads, 'expert', split_axis=0, concat_axis=0, tiled=T...  241 us
    all_to_all x4, waiting for transfers between devices, local(): lax.all_to_all(slot_back.reshape(EXPERTS, CAP, D), 'expert', split_axis=0...  119 us
    ppermute x28, starting transfers between devices, pairwise_exchange(): part = lax.ppermute(part, axis, [(d, d ^ mask) for d in range(ways)])  46.5 us
    scatter x4, local copies, waits for them, and re-layouts, local(): send_grads = jnp.zeros((EXPERTS * CAP, DOUT), jnp.float32).at[slot_place]...  45.7 us
    all_to_all x4, starting transfers between devices, local(): lax.all_to_all(slot_out.reshape(EXPERTS, CAP, DOUT), 'expert', split_axis...  44.2 us
    scatter x4, local copies, waits for them, and re-layouts, local(): send_rows = jnp.zeros((EXPERTS * CAP, D), jnp.float32).at[slot_place].set...  43.9 us
    psum x1, blocking collectives, local(): gate_grad = lax.psum(gate_local, ('dp', 'expert'))  41.1 us
  transfers between devices with their start and end apart: 43, of which 21 were waited for; matrix products, arithmetic and copies ran while one was open for 31% of the time, Pallas kernels for 0%

profile of v1, /device:TPU:0, one launch (start us, length us, event | category | flops | bytes accessed | tf_op | source)
XLA Modules:
  0.0 1444.1 jit_solution(13970313278706490471)
XLA Ops:
  78.6 18.3 %collective-permute-done.11 = f32[2,192,256]{2,1,0:T(8,128)S(1)} collective-permute-done((f32[2,192,256]{2,1,0:T(8,128)S(1)}, f32[2,192,256]{2,1,0:T(8,128)S(1)}, u32[]{:S(2)}, u32[]{:S(2)}) %collective-permute-start.11) | collective-permute-done | bytes 393248 | tf_op jit(solution)/shard_map/ppermute | solution.py:36
  105.3 11.5 all-to-all-start.1
  137.8 11.4 scatter_custom_fusion.2
  158.9 18.2 %collective-permute-done.15 = f32[2,192,256]{2,1,0:T(8,128)S(1)} collective-permute-done((f32[2,192,256]{2,1,0:T(8,128)S(1)}, f32[2,192,256]{2,1,0:T(8,128)S(1)}, u32[]{:S(2)}, u32[]{:S(2)}) %collective-permute-start.15) | collective-permute-done | bytes 393248 | tf_op jit(solution)/shard_map/ppermute | solution.py:36
  189.7 41.3 %collective-permute-done.17 = f32[2,192,256]{2,1,0:T(8,128)S(1)} collective-permute-done((f32[2,192,256]{2,1,0:T(8,128)S(1)}, f32[2,192,256]{2,1,0:T(8,128)S(1)}, u32[]{:S(2)}, u32[]{:S(2)}) %collective-permute-start.17) | collective-permute-done | bytes 393248 | tf_op jit(solution)/shard_map/ppermute | solution.py:36
  231.0 15.9 %collective-permute-done.18 = f32[2,192,256]{2,1,0:T(8,128)S(1)} collective-permute-done((f32[2,192,256]{2,1,0:T(8,128)S(1)}, f32[2,192,256]{2,1,0:T(8,128)S(1)}, u32[]{:S(2)}, u32[]{:S(2)}) %collective-permute-start.18) | collective-permute-done | bytes 393248 | tf_op jit(solution)/shard_map/ppermute | solution.py:36
  287.0 39.4 %collective-permute-done.22 = f32[2,192,256]{2,1,0:T(8,128)S(1)} collective-permute-done((f32[2,192,256]{2,1,0:T(8,128)S(1)}, f32[2,192,256]{2,1,0:T(8,128)S(1)}, u32[]{:S(2)}, u32[]{:S(2)}) %collective-permute-start.22) | collective-permute-done | bytes 393248 | tf_op jit(solution)/shard_map/ppermute | solution.py:36
  334.9 45.4 %collective-permute-done.24 = f32[2,192,256]{2,1,0:T(8,128)S(1)} collective-permute-done((f32[2,192,256]{2,1,0:T(8,128)S(1)}, f32[2,192,256]{2,1,0:T(8,128)S(1)}, u32[]{:S(2)}, u32[]{:S(2)}) %collective-permute-start.24) | collective-permute-done | bytes 393248 | tf_op jit(solution)/shard_map/ppermute | solution.py:36
  380.3 15.9 %collective-permute-done.25 = f32[2,192,256]{2,1,0:T(8,128)S(1)} collective-permute-done((f32[2,192,256]{2,1,0:T(8,128)S(1)}, f32[2,192,256]{2,1,0:T(8,128)S(1)}, u32[]{:S(2)}, u32[]{:S(2)}) %collective-permute-start.25) | collective-permute-done | bytes 393248 | tf_op jit(solution)/shard_map/ppermute | solution.py:36
  436.4 39.3 %collective-permute-done.1 = f32[2,192,256]{2,1,0:T(8,128)S(1)} collective-permute-done((f32[2,192,256]{2,1,0:T(8,128)S(1)}, f32[2,192,256]{2,1,0:T(8,128)S(1)}, u32[]{:S(2)}, u32[]{:S(2)}) %collective-permute-start.1) | collective-permute-done | bytes 393248 | tf_op jit(solution)/shard_map/ppermute | solution.py:36
  484.1 45.4 %collective-permute-done.3 = f32[2,192,256]{2,1,0:T(8,128)S(1)} collective-permute-done((f32[2,192,256]{2,1,0:T(8,128)S(1)}, f32[2,192,256]{2,1,0:T(8,128)S(1)}, u32[]{:S(2)}, u32[]{:S(2)}) %collective-permute-start.3) | collective-permute-done | bytes 393248 | tf_op jit(solution)/shard_map/ppermute | solution.py:36
  529.5 15.9 %collective-permute-done.4 = f32[2,192,256]{2,1,0:T(8,128)S(1)} collective-permute-done((f32[2,192,256]{2,1,0:T(8,128)S(1)}, f32[2,192,256]{2,1,0:T(8,128)S(1)}, u32[]{:S(2)}, u32[]{:S(2)}) %collective-permute-start.4) | collective-permute-done | bytes 393248 | tf_op jit(solution)/shard_map/ppermute | solution.py:36
  693.9 11.5 scatter_custom_fusion.7
  710.8 11.4 scatter_custom_fusion.6
  722.2 60.1 %all-to-all-done.10 = f32[16,192,256]{2,1,0:T(8,128)S(1)} async-done(((f32[16,192,256]{2,1,0:T(8,128)}), f32[16,192,256]{2,1,0:T(8,128)S(1)}, u32[]{:S(2)}, u32[]{:S(2)}) %all-to-all-start.10) | async-done | bytes 3145760 | tf_op jit(solution)/shard_map/all_to_all | solution.py:171
  788.5 11.4 scatter_custom_fusion.4
  799.9 60.1 %all-to-all-done.8 = f32[16,192,256]{2,1,0:T(8,128)} async-done(((f32[16,192,256]{2,1,0:T(8,128)}), f32[16,192,256]{2,1,0:T(8,128)}, u32[]{:S(2)}, u32[]{:S(2)}) %all-to-all-start.8) | async-done | bytes 3145760 | tf_op jit(solution)/shard_map/all_to_all | solution.py:171
  863.7 11.5 scatter_custom_fusion.5
  875.1 60.0 %all-to-all-done.4 = f32[16,192,256]{2,1,0:T(8,128)S(1)} async-done(((f32[16,192,256]{2,1,0:T(8,128)}), f32[16,192,256]{2,1,0:T(8,128)S(1)}, u32[]{:S(2)}, u32[]{:S(2)}) %all-to-all-start.4) | async-done | bytes 3145760 | tf_op jit(solution)/shard_map/all_to_all | solution.py:171
  952.8 60.8 %all-to-all-done.6 = f32[16,192,256]{2,1,0:T(8,128)} async-done(((f32[16,192,256]{2,1,0:T(8,128)}), f32[16,192,256]{2,1,0:T(8,128)}, u32[]{:S(2)}, u32[]{:S(2)}) %all-to-all-start.6) | async-done | bytes 3145760 | tf_op jit(solution)/shard_map/all_to_all | solution.py:171
  1029.2 59.7 %all-to-all-done.5 = f32[16,192,256]{2,1,0:T(8,128)S(1)} async-done(((f32[16,192,256]{2,1,0:T(8,128)}), f32[16,192,256]{2,1,0:T(8,128)S(1)}, u32[]{:S(2)}, u32[]{:S(2)}) %all-to-all-start.5) | async-done | bytes 3145760 | tf_op jit(solution)/shard_map/all_to_all | solution.py:180
  1105.3 59.8 %all-to-all-done.11 = f32[16,192,256]{2,1,0:T(8,128)} async-done(((f32[16,192,256]{2,1,0:T(8,128)}), f32[16,192,256]{2,1,0:T(8,128)}, u32[]{:S(2)}, u32[]{:S(2)}) %all-to-all-start.11) | async-done | bytes 3145760 | tf_op jit(solution)/shard_map/all_to_all | solution.py:180
  1239.3 41.1 %psum.7 = f32[256,40]{0,1:T(8,128)S(1)} all-reduce(f32[256,40]{0,1:T(8,128)S(1)} %fusion.258), channel_id=1, replica_groups=mesh['dp'=4,'expert'=8] {'dp','expert'}, use_global_device_ids=true, to_apply=%region_36.37 | all-reduce | flops 10240 | bytes 81920 | tf_op jit(solution)/shard_map/psum | solution.py:211
  1370.2 19.4 %reduce-scatter.6.cloned.1.call-done = f32[2,64,256]{2,1,0:T(8,128)} async-done(((f32[2,256,256]{2,1,0:T(8,128)}), f32[2,64,256]{2,1,0:T(8,128)}) %reduce-scatter.6.cloned.1.call-update) | async-done | bytes 131088 | tf_op jit(solution)/shard_map/reduce_scatter | solution.py:213
  (527 shorter events, 643.5 us)
Async XLA Ops:
  105.3 150.0 %all-to-all-start.1 = ((f32[16,192,256]{2,1,0:T(8,128)}), f32[16,192,256]{2,1,0:T(8,128)S(1)}, u32[]{:S(2)}, u32[]{:S(2)}) async-start(f32[16,192,256]{2,1,0:T(8,128)} %bitcast.392), calls=%async_computation.1 | async-start | bytes 6291456 | tf_op jit(solution)/shard_map/all_to_all | solution.py:168
  153.6 77.4 %collective-permute-start.17 = (f32[2,192,256]{2,1,0:T(8,128)S(1)}, f32[2,192,256]{2,1,0:T(8,128)S(1)}, u32[]{:S(2)}, u32[]{:S(2)}) collective-permute-start(f32[2,192,256]{2,1,0:T(8,128)S(1)} %get-tuple-element.51), channel_id=1, source_target_pairs={{0,4},{1,5},{2,6},{3,7},{4,0},{5,1},{6,2},{7,3},{8,12},{9,13},{10,... | collective-permute-start | bytes 1179656 | tf_op jit(solution)/shard_map/ppermute | solution.py:36
  156.2 90.8 %collective-permute-start.20 = (f32[2,192,256]{2,1,0:T(8,128)S(1)}, f32[2,192,256]{2,1,0:T(8,128)S(1)}, u32[]{:S(2)}, u32[]{:S(2)}) collective-permute-start(f32[2,192,256]{2,1,0:T(8,128)S(1)} %get-tuple-element.48), channel_id=1, source_target_pairs={{0,7},{1,6},{2,5},{3,4},{4,3},{5,2},{6,1},{7,0},{8,15},{9,14},{10,... | collective-permute-start | bytes 1179656 | tf_op jit(solution)/shard_map/ppermute | solution.py:36
  157.4 89.5 %collective-permute-start.18 = (f32[2,192,256]{2,1,0:T(8,128)S(1)}, f32[2,192,256]{2,1,0:T(8,128)S(1)}, u32[]{:S(2)}, u32[]{:S(2)}) collective-permute-start(f32[2,192,256]{2,1,0:T(8,128)S(1)} %get-tuple-element.50), channel_id=1, source_target_pairs={{0,5},{1,4},{2,7},{3,6},{4,1},{5,0},{6,3},{7,2},{8,13},{9,12},{10,... | collective-permute-start | bytes 1179656 | tf_op jit(solution)/shard_map/ppermute | solution.py:36
  177.1 69.8 %collective-permute-start.19 = (f32[2,192,256]{2,1,0:T(8,128)S(1)}, f32[2,192,256]{2,1,0:T(8,128)S(1)}, u32[]{:S(2)}, u32[]{:S(2)}) collective-permute-start(f32[2,192,256]{2,1,0:T(8,128)S(1)} %get-tuple-element.49), channel_id=1, source_target_pairs={{0,6},{1,7},{2,4},{3,5},{4,2},{5,3},{6,0},{7,1},{8,14},{9,15},{10,... | collective-permute-start | bytes 1179656 | tf_op jit(solution)/shard_map/ppermute | solution.py:36
  255.3 149.3 %all-to-all-start.2 = ((f32[16,192,256]{2,1,0:T(8,128)}), f32[16,192,256]{2,1,0:T(8,128)}, u32[]{:S(2)}, u32[]{:S(2)}) async-start(f32[16,192,256]{2,1,0:T(8,128)} %bitcast.396), calls=%async_computation.2 | async-start | bytes 6291456 | tf_op jit(solution)/shard_map/all_to_all | solution.py:168
  282.8 97.4 %collective-permute-start.24 = (f32[2,192,256]{2,1,0:T(8,128)S(1)}, f32[2,192,256]{2,1,0:T(8,128)S(1)}, u32[]{:S(2)}, u32[]{:S(2)}) collective-permute-start(f32[2,192,256]{2,1,0:T(8,128)S(1)} %get-tuple-element.59), channel_id=1, source_target_pairs={{0,4},{1,5},{2,6},{3,7},{4,0},{5,1},{6,2},{7,3},{8,12},{9,13},{10,... | collective-permute-start | bytes 1179656 | tf_op jit(solution)/shard_map/ppermute | solution.py:36
  284.3 111.9 %collective-permute-start.27 = (f32[2,192,256]{2,1,0:T(8,128)S(1)}, f32[2,192,256]{2,1,0:T(8,128)S(1)}, u32[]{:S(2)}, u32[]{:S(2)}) collective-permute-start(f32[2,192,256]{2,1,0:T(8,128)S(1)} %get-tuple-element.56), channel_id=1, source_target_pairs={{0,7},{1,6},{2,5},{3,4},{4,3},{5,2},{6,1},{7,0},{8,15},{9,14},{10,... | collective-permute-start | bytes 1179656 | tf_op jit(solution)/shard_map/ppermute | solution.py:36
  286.6 109.6 %collective-permute-start.25 = (f32[2,192,256]{2,1,0:T(8,128)S(1)}, f32[2,192,256]{2,1,0:T(8,128)S(1)}, u32[]{:S(2)}, u32[]{:S(2)}) collective-permute-start(f32[2,192,256]{2,1,0:T(8,128)S(1)} %get-tuple-element.58), channel_id=1, source_target_pairs={{0,5},{1,4},{2,7},{3,6},{4,1},{5,0},{6,3},{7,2},{8,13},{9,12},{10,... | collective-permute-start | bytes 1179656 | tf_op jit(solution)/shard_map/ppermute | solution.py:36
  404.5 149.2 %all-to-all-start.3 = ((f32[16,192,256]{2,1,0:T(8,128)}), f32[16,192,256]{2,1,0:T(8,128)}, u32[]{:S(2)}, u32[]{:S(2)}) async-start(f32[16,192,256]{2,1,0:T(8,128)} %bitcast.394), calls=%async_computation.3 | async-start | bytes 6291456 | tf_op jit(solution)/shard_map/all_to_all | solution.py:168
  432.2 97.3 %collective-permute-start.3 = (f32[2,192,256]{2,1,0:T(8,128)S(1)}, f32[2,192,256]{2,1,0:T(8,128)S(1)}, u32[]{:S(2)}, u32[]{:S(2)}) collective-permute-start(f32[2,192,256]{2,1,0:T(8,128)S(1)} %get-tuple-element.35), channel_id=1, source_target_pairs={{0,4},{1,5},{2,6},{3,7},{4,0},{5,1},{6,2},{7,3},{8,12},{9,13},{10,... | collective-permute-start | bytes 1179656 | tf_op jit(solution)/shard_map/ppermute | solution.py:36
  433.8 111.7 %collective-permute-start.6 = (f32[2,192,256]{2,1,0:T(8,128)S(1)}, f32[2,192,256]{2,1,0:T(8,128)S(1)}, u32[]{:S(2)}, u32[]{:S(2)}) collective-permute-start(f32[2,192,256]{2,1,0:T(8,128)S(1)} %get-tuple-element.32), channel_id=1, source_target_pairs={{0,7},{1,6},{2,5},{3,4},{4,3},{5,2},{6,1},{7,0},{8,15},{9,14},{10,... | collective-permute-start | bytes 1179656 | tf_op jit(solution)/shard_map/ppermute | solution.py:36
  436.0 109.4 %collective-permute-start.4 = (f32[2,192,256]{2,1,0:T(8,128)S(1)}, f32[2,192,256]{2,1,0:T(8,128)S(1)}, u32[]{:S(2)}, u32[]{:S(2)}) collective-permute-start(f32[2,192,256]{2,1,0:T(8,128)S(1)} %get-tuple-element.34), channel_id=1, source_target_pairs={{0,5},{1,4},{2,7},{3,6},{4,1},{5,0},{6,3},{7,2},{8,13},{9,12},{10,... | collective-permute-start | bytes 1179656 | tf_op jit(solution)/shard_map/ppermute | solution.py:36
  475.7 69.8 %collective-permute-start.5 = (f32[2,192,256]{2,1,0:T(8,128)S(1)}, f32[2,192,256]{2,1,0:T(8,128)S(1)}, u32[]{:S(2)}, u32[]{:S(2)}) collective-permute-start(f32[2,192,256]{2,1,0:T(8,128)S(1)} %get-tuple-element.33), channel_id=1, source_target_pairs={{0,6},{1,7},{2,4},{3,5},{4,2},{5,3},{6,0},{7,1},{8,14},{9,15},{10,... | collective-permute-start | bytes 1179656 | tf_op jit(solution)/shard_map/ppermute | solution.py:36
  553.8 120.5 %all-to-all-start = ((f32[16,192,256]{2,1,0:T(8,128)}), f32[16,192,256]{2,1,0:T(8,128)}, u32[]{:S(2)}, u32[]{:S(2)}) async-start(f32[16,192,256]{2,1,0:T(8,128)} %bitcast.395), calls=%async_computation | async-start | bytes 6291456 | tf_op jit(solution)/shard_map/all_to_all | solution.py:168
  705.4 76.9 %all-to-all-start.10 = ((f32[16,192,256]{2,1,0:T(8,128)}), f32[16,192,256]{2,1,0:T(8,128)S(1)}, u32[]{:S(2)}, u32[]{:S(2)}) async-start(f32[16,192,256]{2,1,0:T(8,128)} %bitcast.402), calls=%async_computation.10 | async-start | bytes 6291456 | tf_op jit(solution)/shard_map/all_to_all | solution.py:171
  784.0 76.0 %all-to-all-start.8 = ((f32[16,192,256]{2,1,0:T(8,128)}), f32[16,192,256]{2,1,0:T(8,128)}, u32[]{:S(2)}, u32[]{:S(2)}) async-start(f32[16,192,256]{2,1,0:T(8,128)} %bitcast.401), calls=%async_computation.8 | async-start | bytes 6291456 | tf_op jit(solution)/shard_map/all_to_all | solution.py:171
  860.0 75.1 %all-to-all-start.4 = ((f32[16,192,256]{2,1,0:T(8,128)}), f32[16,192,256]{2,1,0:T(8,128)S(1)}, u32[]{:S(2)}, u32[]{:S(2)}) async-start(f32[16,192,256]{2,1,0:T(8,128)} %bitcast.400), calls=%async_computation.4 | async-start | bytes 6291456 | tf_op jit(solution)/shard_map/all_to_all | solution.py:171
  936.9 76.7 %all-to-all-start.6 = ((f32[16,192,256]{2,1,0:T(8,128)}), f32[16,192,256]{2,1,0:T(8,128)}, u32[]{:S(2)}, u32[]{:S(2)}) async-start(f32[16,192,256]{2,1,0:T(8,128)} %bitcast.399), calls=%async_computation.6 | async-start | bytes 6291456 | tf_op jit(solution)/shard_map/all_to_all | solution.py:171
  1013.6 75.3 %all-to-all-start.5 = ((f32[16,192,256]{2,1,0:T(8,128)}), f32[16,192,256]{2,1,0:T(8,128)S(1)}, u32[]{:S(2)}, u32[]{:S(2)}) async-start(f32[16,192,256]{2,1,0:T(8,128)} %bitcast.397), calls=%async_computation.5 | async-start | bytes 6291456 | tf_op jit(solution)/shard_map/all_to_all | solution.py:180
  1088.9 76.2 %all-to-all-start.11 = ((f32[16,192,256]{2,1,0:T(8,128)}), f32[16,192,256]{2,1,0:T(8,128)}, u32[]{:S(2)}, u32[]{:S(2)}) async-start(f32[16,192,256]{2,1,0:T(8,128)} %bitcast.398), calls=%async_computation.11 | async-start | bytes 6291456 | tf_op jit(solution)/shard_map/all_to_all | solution.py:180
  1165.1 126.7 %all-to-all-start.9 = ((f32[16,192,256]{2,1,0:T(8,128)}), f32[16,192,256]{2,1,0:T(8,128)}, u32[]{:S(2)}, u32[]{:S(2)}) async-start(f32[16,192,256]{2,1,0:T(8,128)} %bitcast.393), calls=%async_computation.9 | async-start | bytes 6291456 | tf_op jit(solution)/shard_map/all_to_all | solution.py:180
  1291.7 133.9 %all-to-all-start.7 = ((f32[16,192,256]{2,1,0:T(8,128)}), f32[16,192,256]{2,1,0:T(8,128)}, u32[]{:S(2)}, u32[]{:S(2)}) async-start(f32[16,192,256]{2,1,0:T(8,128)} %bitcast.391), calls=%async_computation.7 | async-start | bytes 6291456 | tf_op jit(solution)/shard_map/all_to_all | solution.py:180
  1296.3 70.6 %reduce-scatter.10.cloned.1.call-start = ((), (), s32[]{:S(2)}) async-start(), calls=%async_computation.17 | async-start | bytes 327680
  (118 other events, 1733.2 us)
Sparse Core Ops, SparseCore 0:
  1306.8 25.2 reduce-scatter.9
  1336.1 25.9 reduce-scatter.7
  1364.9 24.7 reduce-scatter.5
